TPU v7x, 256 devices: a whole 4x4x8 slice. The times are simulated.
256 devices in a mesh: img: 32 (over z, y_hi, core), ori: 8 (over x, y_lo).
Axes of the slice: x: 4, y: 4 (y_hi: 2, y_lo: 2; y = y_hi * 2 + y_lo), z: 8, core: 2. Of those that a mesh axis runs over, the one named last changes fastest.
Arguments:
- images: float32 [32768, 2048], P(('img', 'ori')), may hold values from -40 to 40
- precision: float32 [32768], P('img'), may hold values from 0.5 to 2
- projections: bfloat16 [8192, 2048], P('ori'), may hold values from -1 to 1
- tile_mask: int32 [256, 64], P('img', 'ori'), may hold values from 0 to 1, as said below
Outputs:
- posteriors: bfloat16 [32768, 8192], P('img', 'ori')
- references: float32 [8192, 2048], P(('ori', 'img'))
Inputs may be any that keep to these rules, and one draw needn't show every extreme that they name: `tile_mask`: every image block has at least one live tile.
All inputs are finite; a program needn't handle non-finite values.
Results may differ from a plain program's by a relative error of at most 0.0095.
Values may be sent and summed in bfloat16 or wider, within the bound.
A program may use at most 64 MiB of HBM per device.

v0:
```python
import jax
import jax.numpy as jnp
from jax import lax
from jax.sharding import PartitionSpec as P

prior_weight = 1.0
very_low = -1e30


def weighted_sums(weights, rows_block):
    return lax.dot_general(
        weights, rows_block, (((0,), (0,)), ((), ())), preferred_element_type=jnp.float32
    )


def body(images, precision, projections, tile_mask):
    lowered = images.astype(jnp.bfloat16)
    grouped = lax.all_gather(lowered, "ori", axis=0, tiled=True)
    proj_float = projections.astype(jnp.float32)
    squared = jnp.sum(proj_float * proj_float, axis=1)
    blocks, tiles_here = tile_mask.shape
    per_block = grouped.shape[0] // blocks
    tile_width = projections.shape[0] // tiles_here
    products = lax.dot_general(
        grouped, projections, (((1,), (1,)), ((), ())), preferred_element_type=jnp.float32
    )
    scores = precision[:, None] * (products - 0.5 * squared[None, :])
    shaped = scores.reshape(blocks, per_block, tiles_here, tile_width)
    alive = jnp.broadcast_to((tile_mask > 0)[:, None, :, None], shaped.shape)
    masked = jnp.where(alive, shaped, very_low)
    local_high = jnp.max(masked, axis=(2, 3))
    row_high = lax.pmax(local_high, "ori")
    local_total = jnp.sum(
        jnp.where(alive, jnp.exp(masked - row_high[:, :, None, None]), 0.0), axis=(2, 3)
    )
    row_total = lax.psum(local_total, "ori")
    probable = (
        jnp.where(alive, jnp.exp(masked - row_high[:, :, None, None]), 0.0)
        / row_total[:, :, None, None]
    )
    posteriors = probable.reshape(scores.shape).astype(jnp.bfloat16)
    counts = jnp.sum(posteriors.astype(jnp.float32), axis=0)
    summed, totals = (
        lax.psum_scatter(
            weighted_sums(posteriors, grouped), "img", scatter_dimension=0, tiled=True
        ),
        lax.psum_scatter(counts, "img", scatter_dimension=0, tiled=True),
    )
    rows_here = summed.shape[0]
    first_row = lax.axis_index("img") * rows_here
    prior_rows = lax.dynamic_slice_in_dim(proj_float, first_row, rows_here, 0)
    refined = (summed + prior_weight * prior_rows) / (totals[:, None] + prior_weight)
    return (posteriors, refined)


def solution(mesh):
    return jax.shard_map(
        body,
        mesh=mesh,
        in_specs=(P(("img", "ori"), None), P("img"), P("ori", None), P("img", "ori")),
        out_specs=(P("img", "ori"), P(("ori", "img"), None)),
        check_vma=False,
    )
```

profile of v0, /device:TPU:2, one launch (start us, length us, event | category | flops | bytes accessed | tf_op | source)
XLA Modules:
  0.0 328.1 jit_solution(5797426212921994888)
XLA Ops:
  7.2 0.0 copy-start
  7.2 0.0 all-gather.2.cloned.1.call-start
  7.2 2.1 convert_element_type.12
  9.3 0.0 all-gather.2.cloned.1.call-update
  9.3 0.0 reduce-scatter.2.cloned.1.call-start
  9.4 0.7 broadcast_compare_fusion
  10.1 0.1 copy.8
  10.2 3.1 multiply_reduce_fusion
  13.2 92.3 %all-gather.2.cloned.1.call-done = bf16[1024,2048]{1,0:T(8,128)(2,1)} async-done(((bf16[128,2048]{1,0:T(8,128)(2,1)}), bf16[1024,2048]{1,0:T(8,128)(2,1)}) %all-gather.2.cloned.1.call-update) | async-done | bytes 4194320 | tf_op jit(solution)/shard_map/all_gather | solution.py:18
  105.5 0.3 broadcast_in_dim.22
  105.9 0.0 copy-done
  105.9 10.2 %fusion = (f32[1024]{0:T(1024)S(1)}, f32[1024,1024]{0,1:T(8,128)}) fusion(pred[128,8,8,128]{3,2,1,0:T(8,128)(4,1)S(1)} %bitcast.21, f32[1024]{0:T(1024)S(1)} %broadcast_multiply_fusion, f32[1024]{0:T(1024)S(1)} %copy-done, bf16[1024,2048]{1,0:T(8,128)(2,1)} %all-gather.2.cloned.1.call-done, bf16[1024,2048]{1,0:T(8,128)(2,1)} %param.6), kind=kOutput, calls=%fused_computation.5 | convolution fusion | flops 4299160576 | bytes 13643776 | tf_op jit(solution)/shard_map/dot_general | solution.py:24
  116.1 16.3 %pmax.7 = f32[1024]{0:T(1024)S(1)} all-reduce(f32[1024]{0:T(1024)S(1)} %get-tuple-element.8), channel_id=1, replica_groups=mesh['img'=32,'ori'=8] {'ori'}, use_global_device_ids=true, to_apply=%region_2.3 | all-reduce | flops 1024 | bytes 8192 | tf_op jit(solution)/shard_map/pmax | solution.py:32
  132.4 3.7 %fusion.1 = f32[1024]{0:T(1024)S(1)} fusion(f32[1024]{0:T(1024)S(1)} %pmax.7, f32[1024,1024]{0,1:T(8,128)} %get-tuple-element.9, f32[1024]{0:T(1024)S(1)} %broadcast_multiply_fusion, f32[1024]{0:T(1024)S(1)} %copy-done, pred[128,8,8,128]{3,2,1,0:T(8,128)(4,1)S(1)} %bitcast.22), kind=kLoop, calls=%fused_computation.6 | loop fusion | flops 6290432 | bytes 5259264 | tf_op jit(solution)/shard_map/reduce_sum | solution.py:33
  136.1 16.0 %psum.7 = f32[1024]{0:T(1024)S(1)} all-reduce(f32[1024]{0:T(1024)S(1)} %fusion.1), channel_id=1, replica_groups=mesh['img'=32,'ori'=8] {'ori'}, use_global_device_ids=true, to_apply=%region_4.5 | all-reduce | flops 1024 | bytes 8192 | tf_op jit(solution)/shard_map/psum | solution.py:36
  152.0 0.0 copy-start.1
  152.0 4.0 %convert_reduce_fusion = (f32[1024]{0:T(1024)S(1)}, bf16[1024,1024]{0,1:T(8,128)(2,1)S(1)}) fusion(f32[1024]{0:T(1024)S(1)} %psum.7, f32[1024]{0:T(1024)S(1)} %pmax.7, f32[1024,1024]{0,1:T(8,128)} %get-tuple-element.9, f32[1024]{0:T(1024)S(1)} %broadcast_multiply_fusion, f32[1024]{0:T(1024)S(1)} %copy-done, pred[128,8,8,128]{3,2,1,0:T(8,128)(4,1)S(1)} %bitcast.23), kind=kLoop, calls=%fused_computation.1 | loop fusion | flops 9436160 | bytes 7360512 | tf_op jit(solution)/shard_map/reduce_sum | solution.py:42
  156.0 0.0 copy-done.1
  156.0 6.6 %fusion.2 = f32[1024,2048]{1,0:T(8,128)} fusion(bf16[1024,1024]{0,1:T(8,128)(2,1)S(1)} %get-tuple-element.7, bf16[1024,2048]{1,0:T(8,128)(2,1)S(1)} %copy-done.1), kind=kOutput, calls=%fused_computation.11 | convolution fusion | flops 4294967296 | bytes 14680064 | tf_op jit(solution)/shard_map/dot_general | solution.py:11
  162.7 0.0 reduce-scatter.2.cloned.1.call-update
  162.7 0.0 copy-start.2
  162.7 6.5 %convert_element_type.13 = f32[1024,2048]{1,0:T(8,128)} convert(bf16[1024,2048]{1,0:T(8,128)(2,1)} %param.6) | non-fusion elementwise | flops 2097152 | bytes 12582912 | tf_op jit(solution)/shard_map/convert_element_type | solution.py:19
  169.2 0.0 copy-done.2
  169.2 0.6 dynamic-slice
  170.4 2.6 copy.9
  173.0 65.6 %all-reduce = f32[1024]{0:T(1024)S(1)} all-reduce(f32[1024]{0:T(1024)S(1)} %get-tuple-element.6), channel_id=3, replica_groups=mesh['img'=32,'ori'=8] {'img'}, use_global_device_ids=true, to_apply=%region_7.8.clone | all-reduce | flops 1024 | bytes 8192
  238.6 0.1 dynamic-slice_add_fusion
  238.6 80.8 %reduce-scatter.2.cloned.1.call-done = f32[32,2048]{1,0:T(8,128)} async-done(((f32[1024,2048]{1,0:T(8,128)}), f32[32,2048]{1,0:T(8,128)}) %reduce-scatter.2.cloned.1.call-update) | async-done | bytes 262160 | tf_op jit(solution)/shard_map/reduce_scatter | solution.py:44
  319.4 1.8 add_divide_fusion
  (1 shorter events, 0.0 us)
Async XLA Ops:
  7.2 98.7 %copy-start = (f32[1024]{0:T(1024)S(1)}, f32[1024]{0:T(1024)}, u32[]{:S(2)}) copy-start(f32[1024]{0:T(1024)} %param.5) | copy-start | bytes 12292
  7.2 98.4 %all-gather.2.cloned.1.call-start = ((), (), s32[]{:S(2)}) async-start(), calls=%async_computation.1 | async-start | bytes 4718592 | tf_op jit(solution)/shard_map/all_gather | solution.py:18
  9.3 310.1 %reduce-scatter.2.cloned.1.call-start = ((), (), s32[]{:S(2)}) async-start(), calls=%async_computation.2 | async-start | bytes 8650752 | tf_op jit(solution)/shard_map/reduce_scatter | solution.py:44
  152.0 4.0 %copy-start.1 = (bf16[1024,2048]{1,0:T(8,128)(2,1)S(1)}, bf16[1024,2048]{1,0:T(8,128)(2,1)}, u32[]{:S(2)}) copy-start(bf16[1024,2048]{1,0:T(8,128)(2,1)} %all-gather.2.cloned.1.call-done) | copy-start | bytes 12582916
  162.7 6.5 %copy-start.2 = (u32[256]{0:T(256)S(1)}, u32[256]{0:T(256)}, u32[]{:S(2)}) copy-start(u32[256]{0:T(256)} %constant.27) | copy-start | bytes 3076
Sparse Core Ops, SparseCore 0:
  10.3 95.1 all-gather.1
  162.8 156.5 reduce-scatter.1
where the time goes:
time: 328 us
  waiting for transfers between devices  173 us (53%)
  blocking collectives  97.8 us (30%)
  other arithmetic  21.9 us (7%)
  matrix products  16.8 us (5%)
  between operations  14.8 us (5%)
  local copies, waits for them, and re-layouts  3.58 us (1%)
    all_gather x1, waiting for transfers between devices, body(): grouped = lax.all_gather(lowered, 'ori', axis=0, tiled=True)  92.3 us
    reduce_scatter x1, waiting for transfers between devices, body(): lax.psum_scatter(weighted_sums(posteriors, grouped), 'img', scatter_dimen...  80.8 us
    unnamed x1, blocking collectives  65.6 us
    pmax x1, blocking collectives, body(): row_high = lax.pmax(local_high, 'ori')  16.3 us
    psum x1, blocking collectives, body(): row_total = lax.psum(local_total, 'ori')  16 us
    dot_general x1, matrix products, body(): lax.dot_general(grouped, projections, (((1,), (1,)), ((), ())), preferred...  10.2 us
    dot_general x1, matrix products, weighted_sums(): lax.dot_general(weights, rows_block, (((0,), (0,)), ((), ())), preferred_...  6.65 us
  transfers between devices with their start and end apart: 2, of which 2 were waited for; matrix products, arithmetic and copies ran while one was open for 4% of the time, Pallas kernels for 0%

commit v1 on v0

--- a/solution.py
+++ b/solution.py
@@ -15,7 +15,9 @@
 
 def body(images, precision, projections, tile_mask):
     lowered = images.astype(jnp.bfloat16)
-    grouped = lax.all_gather(lowered, "ori", axis=0, tiled=True)
+    grouped = jnp.concatenate(
+        lax.all_to_all(jnp.stack([lowered] * lax.axis_size("ori")), "ori", 0, 0), axis=0
+    )
     proj_float = projections.astype(jnp.float32)
     squared = jnp.sum(proj_float * proj_float, axis=1)
     blocks, tiles_here = tile_mask.shape

time: 328 us -> 302 us (0.921)
  waiting for transfers between devices: 173 us -> 132 us
  starting transfers between devices: 0.08 us -> 6.86 us
  blocking collectives: 97.8 us -> 103 us
    all_gather x1 -> x0, waiting for transfers between devices: 92.3 us -> none  [body(): grouped = lax.all_gather(lowered, 'ori', axis=0, tiled=True)]
    all_to_all x0 -> x1, waiting for transfers between devices: none -> 52.1 us  [body(): lax.all_to_all(jnp.stack([lowered] * lax.axis_size('ori')), 'ori', 0, 0)]
    all_to_all x0 -> x1, starting transfers between devices: none -> 6.85 us  [body(): lax.all_to_all(jnp.stack([lowered] * lax.axis_size('ori')), 'ori', 0, 0)]
where the time goes in v1:
time: 302 us; the launch traced here: 301 us
  waiting for transfers between devices  132 us (44%)
  blocking collectives  103 us (34%)
  other arithmetic  20.3 us (7%)
  matrix products  19 us (6%)
  between operations  14.8 us (5%)
  starting transfers between devices  6.86 us (2%)
  local copies, waits for them, and re-layouts  6.04 us (2%)
    reduce_scatter x1, waiting for transfers between devices, body(): lax.psum_scatter(weighted_sums(posteriors, grouped), 'img', scatter_dimen...  79.8 us
    unnamed x1, blocking collectives  67.9 us
    all_to_all x1, waiting for transfers between devices, body(): lax.all_to_all(jnp.stack([lowered] * lax.axis_size('ori')), 'ori', 0, 0)  52.1 us
    pmax x1, blocking collectives, body(): row_high = lax.pmax(local_high, 'ori')  17.4 us
    psum x1, blocking collectives, body(): row_total = lax.psum(local_total, 'ori')  17.2 us
    dot_general x1, matrix products, body(): lax.dot_general(grouped, projections, (((1,), (1,)), ((), ())), preferred...  10.1 us
    dot_general x1, matrix products, weighted_sums(): lax.dot_general(weights, rows_block, (((0,), (0,)), ((), ())), preferred_...  8.86 us
    all_to_all x1, starting transfers between devices, body(): lax.all_to_all(jnp.stack([lowered] * lax.axis_size('ori')), 'ori', 0, 0)  6.85 us
  transfers between devices with their start and end apart: 2, of which 2 were waited for; matrix products, arithmetic and copies ran while one was open for 4% of the time, Pallas kernels for 0%

profile of v1, /device:TPU:2, one launch (start us, length us, event | category | flops | bytes accessed | tf_op | source)
XLA Modules:
  0.0 301.4 jit_solution(15294209598058272453)
XLA Ops:
  7.2 1.3 convert_element_type.12
  8.5 2.5 stack.2
  10.9 0.0 copy-start.1
  10.9 6.9 %all-to-all-start = ((bf16[8,128,2048]{2,1,0:T(8,128)(2,1)}), bf16[8,128,2048]{2,1,0:T(8,128)(2,1)}, u32[]{:S(2)}, u32[]{:S(2)}) async-start(bf16[8,128,2048]{2,1,0:T(8,128)(2,1)} %stack.2), calls=%async_computation | async-start | bytes 8388608 | tf_op jit(solution)/shard_map/all_to_all | solution.py:19
  17.8 0.0 copy-start
  17.8 0.0 reduce-scatter.2.cloned.1.call-start
  17.8 0.0 copy-done.1
  17.8 0.1 copy.8
  17.9 3.1 %multiply_reduce_fusion = f32[1024]{0:T(1024)S(1)} fusion(bf16[1024,2048]{1,0:T(8,128)(2,1)} %param.6), kind=kLoop, calls=%fused_computation | loop fusion | flops 6290432 | bytes 4198400 | tf_op jit(solution)/shard_map/reduce_sum | solution.py:22
  21.0 52.1 %all-to-all-done = bf16[8,128,2048]{2,1,0:T(8,128)(2,1)} async-done(((bf16[8,128,2048]{2,1,0:T(8,128)(2,1)}), bf16[8,128,2048]{2,1,0:T(8,128)(2,1)}, u32[]{:S(2)}, u32[]{:S(2)}) %all-to-all-start) | async-done | bytes 4194336 | tf_op jit(solution)/shard_map/all_to_all | solution.py:19
  73.1 0.3 broadcast_in_dim.22
  73.4 0.0 copy-done
  73.4 10.1 %fusion = (f32[1024]{0:T(1024)S(1)}, f32[1024,1024]{0,1:T(8,128)}) fusion(pred[128,8,8,128]{3,2,1,0:T(8,128)(4,1)S(1)} %bitcast.22, f32[1024]{0:T(1024)S(1)} %broadcast_multiply_fusion, f32[1024]{0:T(1024)S(1)} %copy-done, bf16[1024,2048]{1,0:T(8,128)(2,1)} %bitcast, bf16[1024,2048]{1,0:T(8,128)(2,1)} %param.6), kind=kOutput, calls=%fused_computation.5 | convolution fusion | flops 4299160576 | bytes 13643776 | tf_op jit(solution)/shard_map/dot_general | solution.py:26
  83.6 17.4 %pmax.7 = f32[1024]{0:T(1024)S(1)} all-reduce(f32[1024]{0:T(1024)S(1)} %get-tuple-element.8), channel_id=1, replica_groups=mesh['img'=32,'ori'=8] {'ori'}, use_global_device_ids=true, to_apply=%region_2.3 | all-reduce | flops 1024 | bytes 8192 | tf_op jit(solution)/shard_map/pmax | solution.py:34
  101.0 3.7 %fusion.1 = f32[1024]{0:T(1024)S(1)} fusion(f32[1024]{0:T(1024)S(1)} %pmax.7, f32[1024,1024]{0,1:T(8,128)} %get-tuple-element.9, f32[1024]{0:T(1024)S(1)} %broadcast_multiply_fusion, f32[1024]{0:T(1024)S(1)} %copy-done, pred[128,8,8,128]{3,2,1,0:T(8,128)(4,1)S(1)} %bitcast.23), kind=kLoop, calls=%fused_computation.6 | loop fusion | flops 6290432 | bytes 5259264 | tf_op jit(solution)/shard_map/reduce_sum | solution.py:35
  104.7 17.2 %psum.7 = f32[1024]{0:T(1024)S(1)} all-reduce(f32[1024]{0:T(1024)S(1)} %fusion.1), channel_id=1, replica_groups=mesh['img'=32,'ori'=8] {'ori'}, use_global_device_ids=true, to_apply=%region_4.5 | all-reduce | flops 1024 | bytes 8192 | tf_op jit(solution)/shard_map/psum | solution.py:38
  121.9 3.8 %convert_reduce_fusion = (f32[1024]{0:T(1024)S(1)}, bf16[1024,1024]{0,1:T(8,128)(2,1)S(1)}) fusion(f32[1024]{0:T(1024)S(1)} %psum.7, f32[1024]{0:T(1024)S(1)} %pmax.7, f32[1024,1024]{0,1:T(8,128)} %get-tuple-element.9, f32[1024]{0:T(1024)S(1)} %broadcast_multiply_fusion, f32[1024]{0:T(1024)S(1)} %copy-done, pred[128,8,8,128]{3,2,1,0:T(8,128)(4,1)S(1)} %bitcast.24), kind=kLoop, calls=%fused_computation.1 | loop fusion | flops 9436160 | bytes 7360512 | tf_op jit(solution)/shard_map/reduce_sum | solution.py:44
  125.7 8.9 %fusion.2 = f32[1024,2048]{1,0:T(8,128)} fusion(bf16[1024,1024]{0,1:T(8,128)(2,1)S(1)} %get-tuple-element.7, bf16[1024,2048]{1,0:T(8,128)(2,1)} %bitcast), kind=kOutput, calls=%fused_computation.11 | convolution fusion | flops 4294967296 | bytes 14680064 | tf_op jit(solution)/shard_map/dot_general | solution.py:11
  134.6 0.0 reduce-scatter.2.cloned.1.call-update
  134.6 0.0 copy-start.2
  134.7 6.5 %convert_element_type.13 = f32[1024,2048]{1,0:T(8,128)} convert(bf16[1024,2048]{1,0:T(8,128)(2,1)} %param.6) | non-fusion elementwise | flops 2097152 | bytes 12582912 | tf_op jit(solution)/shard_map/convert_element_type | solution.py:21
  141.1 0.0 copy-done.2
  141.1 0.6 dynamic-slice
  142.4 2.6 copy.9
  144.9 67.9 %all-reduce = f32[1024]{0:T(1024)S(1)} all-reduce(f32[1024]{0:T(1024)S(1)} %get-tuple-element.6), channel_id=3, replica_groups=mesh['img'=32,'ori'=8] {'img'}, use_global_device_ids=true, to_apply=%region_7.8.clone | all-reduce | flops 1024 | bytes 8192
  212.9 0.1 dynamic-slice_add_fusion
  212.9 79.8 %reduce-scatter.2.cloned.1.call-done = f32[32,2048]{1,0:T(8,128)} async-done(((f32[1024,2048]{1,0:T(8,128)}), f32[32,2048]{1,0:T(8,128)}) %reduce-scatter.2.cloned.1.call-update) | async-done | bytes 262160 | tf_op jit(solution)/shard_map/reduce_scatter | solution.py:46
  292.7 1.8 add_divide_fusion
  (2 shorter events, 0.0 us)
Async XLA Ops:
  10.9 6.9 %copy-start.1 = (s32[8,8]{1,0:T(8,128)S(1)}, s32[8,8]{1,0:T(8,128)}, u32[]{:S(2)}) copy-start(s32[8,8]{1,0:T(8,128)} %param.7) | copy-start | bytes 772
  10.9 62.2 %all-to-all-start = ((bf16[8,128,2048]{2,1,0:T(8,128)(2,1)}), bf16[8,128,2048]{2,1,0:T(8,128)(2,1)}, u32[]{:S(2)}, u32[]{:S(2)}) async-start(bf16[8,128,2048]{2,1,0:T(8,128)(2,1)} %stack.2), calls=%async_computation | async-start | bytes 8388608 | tf_op jit(solution)/shard_map/all_to_all | solution.py:19
  17.8 55.7 %copy-start = (f32[1024]{0:T(1024)S(1)}, f32[1024]{0:T(1024)}, u32[]{:S(2)}) copy-start(f32[1024]{0:T(1024)} %param.5) | copy-start | bytes 12292
  17.8 274.9 %reduce-scatter.2.cloned.1.call-start = ((), (), s32[]{:S(2)}) async-start(), calls=%async_computation.2 | async-start | bytes 8650752 | tf_op jit(solution)/shard_map/reduce_scatter | solution.py:46
  134.6 6.5 %copy-start.2 = (u32[256]{0:T(256)S(1)}, u32[256]{0:T(256)}, u32[]{:S(2)}) copy-start(u32[256]{0:T(256)} %constant.27) | copy-start | bytes 3076
Sparse Core Ops, SparseCore 0:
  134.8 157.8 reduce-scatter.1
